TPU v7x, 128 devices: a whole 4x4x4 slice. The times are simulated.
128 devices in a mesh: expert: 16 (over y, x_lo, core), tensor: 8 (over x_hi, z).
Axes of the slice: x: 4 (x_hi: 2, x_lo: 2; x = x_hi * 2 + x_lo), y: 4, z: 4, core: 2. Of those that a mesh axis runs over, the one named last changes fastest.
Arguments:
- tokens: bfloat16 [4096, 7168], P(('expert', 'tensor')), may hold values from -6 to 6
- expert_ids: int32 [4096, 2], P('expert'), may hold values from 0 to 2, all different within a row
- gate_scores: int32 [4096, 2], P('expert'), may hold values from 1 to 64
- gate_weight: bfloat16 [3, 7168, 2048], P(None, ('expert', 'tensor')), may hold values from -0.0625 to 0.0625
- up_weight: bfloat16 [3, 7168, 2048], P(None, ('expert', 'tensor')), may hold values from -0.0625 to 0.0625
- down_weight: bfloat16 [3, 7168, 2048], P(None, ('expert', 'tensor')), may hold values from -0.1875 to 0.1875
Outputs:
- mixed: bfloat16 [4096, 7168], P(('expert', 'tensor'))
Inputs may be any that keep to these rules, and one draw needn't show every extreme that they name: `expert_ids`: each row names 2 different experts.
All inputs are finite; a program needn't handle non-finite values.
Results may differ from a plain program's by a relative error of at most 0.015.
Values may be sent and summed in bfloat16 or wider, within the bound.
A program may use at most 128 MiB of HBM per device.

v0:
```python
import jax
import jax.numpy as jnp
from jax import lax
from jax.sharding import PartitionSpec as P


def activate(gate_sum, up_sum, weight_col):
    return (jax.nn.silu(gate_sum) * up_sum * weight_col).astype(jnp.bfloat16)


def local(tokens, expert_ids, gate_scores, gate_weight, up_weight, down_weight):
    gathered = lax.all_gather(tokens, "tensor", axis=0, tiled=True)
    experts = gate_weight.shape[0]
    scores = gate_scores.astype(jnp.float32)
    score_sum = jnp.sum(scores, axis=1, keepdims=True)
    labels = jnp.arange(experts, dtype=jnp.int32)
    picked = (expert_ids[:, :, None] == labels[None, None, :]).astype(jnp.float32)
    combine = jnp.sum(scores[:, :, None] * picked, axis=1) / score_sum
    served_gate, served_up, served_down = (
        lax.all_to_all(gate_weight, "tensor", split_axis=2, concat_axis=1, tiled=True),
        lax.all_to_all(up_weight, "tensor", split_axis=2, concat_axis=1, tiled=True),
        lax.all_to_all(down_weight, "tensor", split_axis=2, concat_axis=1, tiled=True),
    )
    hiddens = []
    full_gate, full_up = (
        lax.all_gather(served_gate, "expert", axis=1, tiled=True),
        lax.all_gather(served_up, "expert", axis=1, tiled=True),
    )
    for which in range(experts):
        gate_sum = jnp.dot(gathered, full_gate[which], preferred_element_type=jnp.float32)
        up_sum = jnp.dot(gathered, full_up[which], preferred_element_type=jnp.float32)
        hiddens.append(activate(gate_sum, up_sum, combine[:, which : which + 1]))
    stacked = jnp.stack(hiddens)
    partial_sum = jnp.einsum(
        "etf,edf->td",
        stacked,
        lax.all_gather(served_down, "expert", axis=1, tiled=True),
        preferred_element_type=jnp.float32,
    )
    output_rows = lax.psum_scatter(
        partial_sum.astype(jnp.bfloat16), "tensor", scatter_dimension=0, tiled=True
    )
    return output_rows


def solution(mesh):
    return jax.shard_map(
        local,
        mesh=mesh,
        in_specs=(
            P(("expert", "tensor"), None),
            P("expert", None),
            P("expert", None),
            P(None, ("expert", "tensor"), None),
            P(None, ("expert", "tensor"), None),
            P(None, ("expert", "tensor"), None),
        ),
        out_specs=P(("expert", "tensor"), None),
        check_vma=False,
    )
```

profile of v0, /device:TPU:0, one launch (start us, length us, event | category | flops | bytes accessed | tf_op | source)
XLA Modules:
  0.0 393.2 jit_solution(62899333029683740)
XLA Ops:
  7.3 2.8 copy.28
  10.1 2.7 reshape.8
  12.8 25.9 %all_to_all.54 = bf16[8,2,21504]{2,1,0:T(2,128)(2,1)S(1)} all-to-all(bf16[8,2,21504]{2,1,0:T(2,128)(2,1)S(1)} %reshape.8), channel_id=1, replica_groups=mesh['expert'=16,'tensor'=8] {'tensor'}, dimensions={0} | all-to-all | bytes 1376256 | tf_op jit(solution)/shard_map/all_to_all | solution.py:20
  38.8 3.0 reshape.9
  41.8 2.1 copy.37
  45.4 2.7 reshape.6
  48.1 20.4 %all_to_all.55 = bf16[8,2,21504]{2,1,0:T(2,128)(2,1)S(1)} all-to-all(bf16[8,2,21504]{2,1,0:T(2,128)(2,1)S(1)} %reshape.6), channel_id=1, replica_groups=mesh['expert'=16,'tensor'=8] {'tensor'}, dimensions={0} | all-to-all | bytes 1376256 | tf_op jit(solution)/shard_map/all_to_all | solution.py:21
  68.5 3.0 reshape.7
  71.5 2.2 copy.39
  75.1 2.7 reshape.4
  77.9 14.4 %all_to_all.56 = bf16[8,2,21504]{2,1,0:T(2,128)(2,1)S(1)} all-to-all(bf16[8,2,21504]{2,1,0:T(2,128)(2,1)S(1)} %reshape.4), channel_id=1, replica_groups=mesh['expert'=16,'tensor'=8] {'tensor'}, dimensions={0} | all-to-all | bytes 1376256 | tf_op jit(solution)/shard_map/all_to_all | solution.py:22
  92.2 3.0 reshape.5
  95.2 2.2 copy.35
  97.8 58.9 %all-gather.7.cloned.1.call-done = bf16[3,7168,256]{2,1,0:T(8,128)(2,1)} async-done(((bf16[3,448,256]{2,1,0:T(8,128)(2,1)}), bf16[3,7168,256]{2,1,0:T(8,128)(2,1)}) %all-gather.7.cloned.1.call-update) | async-done | bytes 11010064 | tf_op jit(solution)/shard_map/all_gather | solution.py:26
  156.7 4.4 %fusion.2 = f32[256,256]{1,0:T(8,128)S(1)} fusion(bf16[256,7168]{1,0:T(8,128)(2,1)} %all-gather.5.cloned.1.call-done, bf16[3,7168,256]{2,1,0:T(8,128)(2,1)} %all-gather.7.cloned.1.call-done), kind=kOutput, calls=%fused_computation.5 | convolution fusion | flops 939524096 | bytes 7602176 | tf_op jit(solution)/shard_map/dot_general | solution.py:30
  161.1 3.2 fusion.4
  164.3 3.2 fusion.6
  167.6 56.2 %all-gather.9.cloned.1.call-done = bf16[3,7168,256]{2,1,0:T(8,128)(2,1)} async-done(((bf16[3,448,256]{2,1,0:T(8,128)(2,1)}), bf16[3,7168,256]{2,1,0:T(8,128)(2,1)}) %all-gather.9.cloned.1.call-update) | async-done | bytes 11010064 | tf_op jit(solution)/shard_map/all_gather | solution.py:27
  223.8 4.4 %fusion.18 = bf16[1,256,256]{2,1,0:T(8,128)(2,1)S(1)} fusion(bf16[256,7168]{1,0:T(8,128)(2,1)} %all-gather.5.cloned.1.call-done, bf16[3,7168,256]{2,1,0:T(8,128)(2,1)} %all-gather.9.cloned.1.call-done, f32[256,256]{1,0:T(8,128)S(1)} %fusion.2, f32[256]{0:T(256)S(1)} %bitcast.93), kind=kOutput, calls=%fused_computation.25 | convolution fusion | flops 939982848 | bytes 7734272 | tf_op jit(solution)/shard_map/dot_general | solution.py:31
  228.2 3.2 fusion.17
  231.4 3.2 fusion.16
  234.6 56.2 %all-gather.11.cloned.1.call-done = bf16[3,7168,256]{2,1,0:T(8,128)(2,1)} async-done(((bf16[3,448,256]{2,1,0:T(8,128)(2,1)}), bf16[3,7168,256]{2,1,0:T(8,128)(2,1)}) %all-gather.11.cloned.1.call-update) | async-done | bytes 11010064 | tf_op jit(solution)/shard_map/all_gather | solution.py:37
  290.8 12.7 %fusion = bf16[256,7168]{1,0:T(8,128)(2,1)} fusion(bf16[3,7168,256]{2,1,0:T(8,128)(2,1)} %all-gather.11.cloned.1.call-done, bf16[1,256,256]{2,1,0:T(8,128)(2,1)S(1)} %fusion.18, bf16[1,256,256]{2,1,0:T(8,128)(2,1)S(1)} %fusion.17, bf16[1,256,256]{2,1,0:T(8,128)(2,1)S(1)} %fusion.16), kind=kOutput, calls=%fused_computation.1 | convolution fusion | flops 2820800512 | bytes 15073280 | tf_op jit(solution)/shard_map/etf,edf->td/dot_general | solution.py:34
  303.5 83.2 %reduce-scatter.2.cloned.1.call-done = bf16[32,7168]{1,0:T(8,128)(2,1)} async-done(((bf16[256,7168]{1,0:T(8,128)(2,1)}), bf16[32,7168]{1,0:T(8,128)(2,1)}) %reduce-scatter.2.cloned.1.call-update) | async-done | bytes 458768 | tf_op jit(solution)/shard_map/reduce_scatter | solution.py:40
  (30 shorter events, 4.0 us)
Async XLA Ops:
  6.5 91.2 %all-gather.5.cloned.1.call-start = ((), (), s32[]{:S(2)}) async-start(), calls=%async_computation.4 | async-start | bytes 4128768 | tf_op jit(solution)/shard_map/all_gather | solution.py:12
  7.3 149.4 %all-gather.7.cloned.1.call-start = ((), (), s32[]{:S(2)}) async-start(), calls=%async_computation.5 | async-start | bytes 11698176 | tf_op jit(solution)/shard_map/all_gather | solution.py:26
  38.8 5.2 %copy-start = (bf16[3,56,2048]{2,1,0:T(8,128)(2,1)S(1)}, bf16[3,56,2048]{2,1,0:T(8,128)(2,1)}, u32[]{:S(2)}) copy-start(bf16[3,56,2048]{2,1,0:T(8,128)(2,1)} %param.10) | copy-start | bytes 2064388
  44.0 179.8 %all-gather.9.cloned.1.call-start = ((), (), s32[]{:S(2)}) async-start(), calls=%async_computation.6 | async-start | bytes 11698176 | tf_op jit(solution)/shard_map/all_gather | solution.py:27
  68.5 5.3 %copy-start.1 = (bf16[3,56,2048]{2,1,0:T(8,128)(2,1)S(1)}, bf16[3,56,2048]{2,1,0:T(8,128)(2,1)}, u32[]{:S(2)}) copy-start(bf16[3,56,2048]{2,1,0:T(8,128)(2,1)} %param.11) | copy-start | bytes 2064388
  73.7 217.1 %all-gather.11.cloned.1.call-start = ((), (), s32[]{:S(2)}) async-start(), calls=%async_computation.7 | async-start | bytes 11698176 | tf_op jit(solution)/shard_map/all_gather | solution.py:37
  77.8 19.8 %copy-start.2 = (s32[256,2]{0,1:T(2,128)S(1)}, s32[256,2]{0,1:T(2,128)}, u32[]{:S(2)}) copy-start(s32[256,2]{0,1:T(2,128)} %param.8) | copy-start | bytes 6148
  77.9 19.8 %copy-start.3 = (s32[256,2]{0,1:T(2,128)S(1)}, s32[256,2]{0,1:T(2,128)}, u32[]{:S(2)}) copy-start(s32[256,2]{0,1:T(2,128)} %param.7) | copy-start | bytes 6148
  97.4 289.3 %reduce-scatter.2.cloned.1.call-start = ((), (), s32[]{:S(2)}) async-start(), calls=%async_computation.8 | async-start | bytes 4128768 | tf_op jit(solution)/shard_map/reduce_scatter | solution.py:40
  156.7 4.4 %copy-start.4 = (bf16[256,7168]{1,0:T(8,128)(2,1)S(1)}, bf16[256,7168]{1,0:T(8,128)(2,1)}, u32[]{:S(2)}) copy-start(bf16[256,7168]{1,0:T(8,128)(2,1)} %all-gather.5.cloned.1.call-done) | copy-start | bytes 11010052
  223.8 4.4 %copy-start.5 = (bf16[256,7168]{1,0:T(8,128)(2,1)S(1)}, bf16[256,7168]{1,0:T(8,128)(2,1)}, u32[]{:S(2)}) copy-start(bf16[256,7168]{1,0:T(8,128)(2,1)} %all-gather.5.cloned.1.call-done) | copy-start | bytes 11010052
Sparse Core Ops, SparseCore 0:
  9.7 83.9 all-gather.4
  95.3 61.3 all-gather.6
  158.4 65.3 all-gather.8
  225.3 65.3 all-gather.10
  303.6 83.0 reduce-scatter.1
where the time goes:
time: 394 us; the launch traced here: 393 us
  waiting for transfers between devices  255 us (65%)
  blocking collectives  60.7 us (15%)
  matrix products  34.3 us (9%)
  local copies, waits for them, and re-layouts  29.2 us (7%)
  between operations  13.3 us (3%)
    reduce_scatter x1, waiting for transfers between devices, local(): lax.psum_scatter(partial_sum.astype(jnp.bfloat16), 'tensor', scatter_dime...  83.2 us
    all_gather x1, waiting for transfers between devices, local(): lax.all_gather(served_gate, 'expert', axis=1, tiled=True)  58.9 us
    all_gather x1, waiting for transfers between devices, local(): lax.all_gather(served_up, 'expert', axis=1, tiled=True)  56.2 us
    all_gather x1, waiting for transfers between devices, local(): lax.all_gather(served_down, 'expert', axis=1, tiled=True)  56.2 us
    all_to_all x1, blocking collectives, local(): lax.all_to_all(gate_weight, 'tensor', split_axis=2, concat_axis=1, tiled=...  25.9 us
    unnamed x21, local copies, waits for them, and re-layouts  22.7 us
    all_to_all x1, blocking collectives, local(): lax.all_to_all(up_weight, 'tensor', split_axis=2, concat_axis=1, tiled=True)  20.4 us
    all_to_all x1, blocking collectives, local(): lax.all_to_all(down_weight, 'tensor', split_axis=2, concat_axis=1, tiled=...  14.4 us
  transfers between devices with their start and end apart: 5, of which 4 were waited for; matrix products, arithmetic and copies ran while one was open for 13% of the time, Pallas kernels for 0%

commit v1 on v0

--- a/solution.py
+++ b/solution.py
@@ -2,6 +2,13 @@
 import jax.numpy as jnp
 from jax import lax
 from jax.sharding import PartitionSpec as P
+
+
+def exchange_blocks(block, axis, split, join):
+    n_dev = lax.axis_size(axis)
+    pieces = jnp.stack(jnp.split(block, n_dev, axis=split), axis=0)
+    pieces = lax.all_to_all(pieces, axis, split_axis=0, concat_axis=0)
+    return jnp.concatenate(pieces, axis=join)
 
 
 def activate(gate_sum, up_sum, weight_col):
@@ -17,7 +24,7 @@
     picked = (expert_ids[:, :, None] == labels[None, None, :]).astype(jnp.float32)
     combine = jnp.sum(scores[:, :, None] * picked, axis=1) / score_sum
     served_gate, served_up, served_down = (
-        lax.all_to_all(gate_weight, "tensor", split_axis=2, concat_axis=1, tiled=True),
+        exchange_blocks(gate_weight, "tensor", 2, 1),
         lax.all_to_all(up_weight, "tensor", split_axis=2, concat_axis=1, tiled=True),
         lax.all_to_all(down_weight, "tensor", split_axis=2, concat_axis=1, tiled=True),
     )

time: 394 us -> 393 us (level)
    unnamed x21 -> x25, local copies, waits for them, and re-layouts: 22.7 us -> 20.4 us
where the time goes in v1:
time: 393 us
  waiting for transfers between devices  257 us (65%)
  blocking collectives  59.6 us (15%)
  matrix products  35.9 us (9%)
  local copies, waits for them, and re-layouts  26.6 us (7%)
  between operations  13.3 us (3%)
    reduce_scatter x1, waiting for transfers between devices, local(): lax.psum_scatter(partial_sum.astype(jnp.bfloat16), 'tensor', scatter_dime...  83.4 us
    all_gather x1, waiting for transfers between devices, local(): lax.all_gather(served_gate, 'expert', axis=1, tiled=True)  61.9 us
    all_gather x1, waiting for transfers between devices, local(): lax.all_gather(served_up, 'expert', axis=1, tiled=True)  56.2 us
    all_gather x1, waiting for transfers between devices, local(): lax.all_gather(served_down, 'expert', axis=1, tiled=True)  54.7 us
    all_to_all x1, blocking collectives, exchange_blocks(): pieces = lax.all_to_all(pieces, axis, split_axis=0, concat_axis=0)  25.9 us
    unnamed x25, local copies, waits for them, and re-layouts  20.4 us
    all_to_all x1, blocking collectives, local(): lax.all_to_all(up_weight, 'tensor', split_axis=2, concat_axis=1, tiled=True)  19.5 us
    all_to_all x1, blocking collectives, local(): lax.all_to_all(down_weight, 'tensor', split_axis=2, concat_axis=1, tiled=...  14.2 us
  transfers between devices with their start and end apart: 5, of which 4 were waited for; matrix products, arithmetic and copies ran while one was open for 13% of the time, Pallas kernels for 0%

profile of v1, /device:TPU:0, one launch (start us, length us, event | category | flops | bytes accessed | tf_op | source)
XLA Modules:
  0.0 392.8 jit_solution(14080308929781784453)
XLA Ops:
  7.3 0.9 bitcast_dynamic-update-slice_fusion.7
  14.5 25.9 %all_to_all.41 = bf16[8,3,56,256]{3,2,1,0:T(8,128)(2,1)S(1)} all-to-all(bf16[8,3,56,256]{3,2,1,0:T(8,128)(2,1)S(1)} %bitcast_dynamic-update-slice_fusion), channel_id=1, replica_groups=mesh['expert'=16,'tensor'=8] {'tensor'}, dimensions={0} | all-to-all | bytes 1376256 | tf_op jit(solution)/shard_map/all_to_all | solution.py:10
  40.4 0.9 copy.41
  41.4 1.4 copy.42
  42.7 2.7 reshape.14
  45.4 19.5 %all_to_all.42 = bf16[8,2,21504]{2,1,0:T(2,128)(2,1)S(1)} all-to-all(bf16[8,2,21504]{2,1,0:T(2,128)(2,1)S(1)} %reshape.14), channel_id=1, replica_groups=mesh['expert'=16,'tensor'=8] {'tensor'}, dimensions={0} | all-to-all | bytes 1376256 | tf_op jit(solution)/shard_map/all_to_all | solution.py:28
  64.9 3.0 reshape.15
  67.9 2.2 copy.56
  70.2 1.4 copy.48
  71.6 2.7 reshape.12
  74.3 14.2 %all_to_all.43 = bf16[8,2,21504]{2,1,0:T(2,128)(2,1)S(1)} all-to-all(bf16[8,2,21504]{2,1,0:T(2,128)(2,1)S(1)} %reshape.12), channel_id=1, replica_groups=mesh['expert'=16,'tensor'=8] {'tensor'}, dimensions={0} | all-to-all | bytes 1376256 | tf_op jit(solution)/shard_map/all_to_all | solution.py:29
  88.5 3.0 reshape.13
  91.5 2.2 copy.49
  94.0 61.9 %all-gather.5.cloned.1.call-done = bf16[3,7168,256]{2,1,0:T(8,128)(2,1)} async-done(((bf16[3,448,256]{2,1,0:T(8,128)(2,1)}), bf16[3,7168,256]{2,1,0:T(8,128)(2,1)}) %all-gather.5.cloned.1.call-update) | async-done | bytes 11010064 | tf_op jit(solution)/shard_map/all_gather | solution.py:33
  156.0 4.5 %fusion.9 = f32[256,256]{0,1:T(8,128)S(1)} fusion(bf16[256,7168]{1,0:T(8,128)(2,1)} %all-gather.7.cloned.1.call-done, bf16[3,7168,256]{2,1,0:T(8,128)(2,1)} %all-gather.5.cloned.1.call-done), kind=kOutput, calls=%fused_computation.16 | convolution fusion | flops 939524096 | bytes 7602176 | tf_op jit(solution)/shard_map/dot_general | solution.py:37
  160.4 3.2 fusion.8
  163.6 3.2 fusion.7
  166.8 56.2 %all-gather.9.cloned.1.call-done = bf16[3,7168,256]{2,1,0:T(8,128)(2,1)} async-done(((bf16[3,448,256]{2,1,0:T(8,128)(2,1)}), bf16[3,7168,256]{2,1,0:T(8,128)(2,1)}) %all-gather.9.cloned.1.call-update) | async-done | bytes 11010064 | tf_op jit(solution)/shard_map/all_gather | solution.py:34
  223.1 4.8 %fusion.21 = bf16[1,256,256]{1,2,0:T(8,128)(2,1)S(1)} fusion(bf16[256,7168]{1,0:T(8,128)(2,1)} %all-gather.7.cloned.1.call-done, bf16[3,7168,256]{2,1,0:T(8,128)(2,1)} %all-gather.9.cloned.1.call-done, f32[256,256]{0,1:T(8,128)S(1)} %fusion.9, f32[256]{0:T(256)S(1)} %bitcast.115), kind=kOutput, calls=%fused_computation.28 | convolution fusion | flops 939982848 | bytes 7734272 | tf_op jit(solution)/shard_map/dot_general | solution.py:38
  227.9 3.7 fusion.20
  231.6 3.7 fusion.19
  235.4 54.7 %all-gather.11.cloned.1.call-done = bf16[3,7168,256]{2,1,0:T(8,128)(2,1)} async-done(((bf16[3,448,256]{2,1,0:T(8,128)(2,1)}), bf16[3,7168,256]{2,1,0:T(8,128)(2,1)}) %all-gather.11.cloned.1.call-update) | async-done | bytes 11010064 | tf_op jit(solution)/shard_map/all_gather | solution.py:44
  290.0 12.8 %fusion = bf16[256,7168]{1,0:T(8,128)(2,1)} fusion(bf16[3,7168,256]{2,1,0:T(8,128)(2,1)} %all-gather.11.cloned.1.call-done, bf16[1,256,256]{1,2,0:T(8,128)(2,1)S(1)} %fusion.21, bf16[1,256,256]{1,2,0:T(8,128)(2,1)S(1)} %fusion.20, bf16[1,256,256]{1,2,0:T(8,128)(2,1)S(1)} %fusion.19), kind=kOutput, calls=%fused_computation.1 | convolution fusion | flops 2820800512 | bytes 15073280 | tf_op jit(solution)/shard_map/etf,edf->td/dot_general | solution.py:41
  302.9 83.4 %reduce-scatter.2.cloned.1.call-done = bf16[32,7168]{1,0:T(8,128)(2,1)} async-done(((bf16[256,7168]{1,0:T(8,128)(2,1)}), bf16[32,7168]{1,0:T(8,128)(2,1)}) %reduce-scatter.2.cloned.1.call-update) | async-done | bytes 458768 | tf_op jit(solution)/shard_map/reduce_scatter | solution.py:47
  (35 shorter events, 7.5 us)
Async XLA Ops:
  6.5 34.8 %copy-start = (bf16[3,56,2048]{2,1,0:T(8,128)(2,1)S(1)}, bf16[3,56,2048]{2,1,0:T(8,128)(2,1)}, u32[]{:S(2)}) copy-start(bf16[3,56,2048]{2,1,0:T(8,128)(2,1)} %param.10) | copy-start | bytes 2064388
  6.5 87.5 %all-gather.7.cloned.1.call-start = ((), (), s32[]{:S(2)}) async-start(), calls=%async_computation.5 | async-start | bytes 4128768 | tf_op jit(solution)/shard_map/all_gather | solution.py:19
  7.3 148.7 %all-gather.5.cloned.1.call-start = ((), (), s32[]{:S(2)}) async-start(), calls=%async_computation.4 | async-start | bytes 11698176 | tf_op jit(solution)/shard_map/all_gather | solution.py:33
  41.3 181.8 %all-gather.9.cloned.1.call-start = ((), (), s32[]{:S(2)}) async-start(), calls=%async_computation.6 | async-start | bytes 11698176 | tf_op jit(solution)/shard_map/all_gather | solution.py:34
  64.9 5.3 %copy-start.1 = (bf16[3,56,2048]{2,1,0:T(8,128)(2,1)S(1)}, bf16[3,56,2048]{2,1,0:T(8,128)(2,1)}, u32[]{:S(2)}) copy-start(bf16[3,56,2048]{2,1,0:T(8,128)(2,1)} %param.11) | copy-start | bytes 2064388
  70.1 219.9 %all-gather.11.cloned.1.call-start = ((), (), s32[]{:S(2)}) async-start(), calls=%async_computation.7 | async-start | bytes 11698176 | tf_op jit(solution)/shard_map/all_gather | solution.py:44
  74.3 19.7 %copy-start.2 = (s32[256,2]{0,1:T(2,128)S(1)}, s32[256,2]{0,1:T(2,128)}, u32[]{:S(2)}) copy-start(s32[256,2]{0,1:T(2,128)} %param.8) | copy-start | bytes 6148
  74.3 19.7 %copy-start.3 = (s32[256,2]{0,1:T(2,128)S(1)}, s32[256,2]{0,1:T(2,128)}, u32[]{:S(2)}) copy-start(s32[256,2]{0,1:T(2,128)} %param.7) | copy-start | bytes 6148
  93.7 292.6 %reduce-scatter.2.cloned.1.call-start = ((), (), s32[]{:S(2)}) async-start(), calls=%async_computation.8 | async-start | bytes 4128768 | tf_op jit(solution)/shard_map/reduce_scatter | solution.py:47
  156.0 4.5 %copy-start.4 = (bf16[256,7168]{1,0:T(8,128)(2,1)S(1)}, bf16[256,7168]{1,0:T(8,128)(2,1)}, u32[]{:S(2)}) copy-start(bf16[256,7168]{1,0:T(8,128)(2,1)} %all-gather.7.cloned.1.call-done) | copy-start | bytes 11010052
  223.1 4.8 %copy-start.5 = (bf16[256,7168]{1,0:T(8,128)(2,1)S(1)}, bf16[256,7168]{1,0:T(8,128)(2,1)}, u32[]{:S(2)}) copy-start(bf16[256,7168]{1,0:T(8,128)(2,1)} %all-gather.7.cloned.1.call-done) | copy-start | bytes 11010052
Sparse Core Ops, SparseCore 0:
  9.7 82.5 all-gather.6
  93.9 62.0 all-gather.4
  157.6 65.3 all-gather.8
  224.6 65.3 all-gather.10
  303.0 83.2 reduce-scatter.1
